TPU v7x, 256 devices: a whole 4x4x8 slice. The times are simulated.
256 devices in a mesh: section: 16 (over z_lo, y), dp: 16 (over x, z_hi, core).
Axes of the slice: x: 4, y: 4, z: 8 (z_hi: 2, z_lo: 4; z = z_hi * 4 + z_lo), core: 2. Of those that a mesh axis runs over, the one named last changes fastest.
Arguments:
- enc_state: bfloat16 [16, 512, 4096], P('section', 'dp'), may hold values from -1000 to 1000
- final_gain: float32 [4096], replicated, may hold values from 0.5 to 1.5
- queries: bfloat16 [16, 2048, 4096], P('section', 'dp'), may hold values from -60 to 60
- w_key: bfloat16 [16, 4096, 4096], P('section', None, 'dp'), may hold values from -0.09375 to 0.09375
- w_value: bfloat16 [16, 4096, 4096], P('section', None, 'dp'), may hold values from -0.09375 to 0.09375
- ctx_grad: bfloat16 [16, 2048, 4096], P('section', 'dp'), may hold values from -6 to 6
- mem_len: int32 [16], P('dp'), may hold values from 8 to 32, as said below
Outputs:
- query_grad: bfloat16 [16, 2048, 4096], P('section', 'dp')
- key_weight_grad: bfloat16 [16, 4096, 4096], P('section', None, 'dp')
- value_weight_grad: bfloat16 [16, 4096, 4096], P('section', None, 'dp')
- state_grad: bfloat16 [16, 512, 4096], P('section', 'dp')
- gain_grad: float32 [4096], replicated
Inputs may be any that keep to these rules, and one draw needn't show every extreme that they name: Sequence b's memory holds mem_len[b] valid tokens from position 0; in every draw some sequence has all 32.
All inputs are finite; a program needn't handle non-finite values.
Results may differ from a plain program's by a relative error of at most 0.028.
The roundings to bfloat16 on the way count: a program that leaves them out, or rounds other values in their place, can miss the bound.
Values may be sent and summed in bfloat16 or wider, within the bound.
A program may use at most 64 MiB of HBM per device.

v0:
```python
import jax
import jax.numpy as jnp
from jax import lax
from jax.sharding import PartitionSpec as P

HEAD_DIM = 256
epsilon = 1e-06


def broadcast(block, axis, holder):
    block = jnp.where(lax.axis_index(axis) == holder, block, jnp.zeros_like(block))
    return lax.psum(block, axis)


def on_device(enc_state, final_gain, queries, w_key, w_value, ctx_grad, mem_len):
    sections = lax.axis_size("section")
    replicas = lax.axis_size("dp")
    section_index = lax.axis_index("section")
    last_encoder = sections // 2 - 1
    is_decoder = (section_index > last_encoder).astype(jnp.float32)
    is_last = (section_index == last_encoder).astype(jnp.float32)
    src_len = enc_state.shape[1]
    tgt_len = queries.shape[1]
    local_width = w_key.shape[2]
    heads_here = local_width // HEAD_DIM
    score_scale = HEAD_DIM ** (-0.5)
    enc_rows = enc_state[0].astype(jnp.float32)
    inverse = lax.rsqrt(jnp.mean(enc_rows * enc_rows, axis=1, keepdims=True) + epsilon)
    normed = enc_rows * inverse
    memory = (normed * final_gain).astype(jnp.bfloat16)
    sent = broadcast(memory, "section", last_encoder)
    all_memory, all_len = (
        lax.all_gather(sent, "dp", axis=0, tiled=True),
        lax.all_gather(mem_len, "dp", axis=0, tiled=True),
    )
    w_both = jnp.concatenate([w_key[0], w_value[0]], axis=1)
    projected = jnp.dot(all_memory, w_both, preferred_element_type=jnp.float32).astype(jnp.bfloat16)
    key_rows = projected[:, :local_width].reshape(replicas, src_len, heads_here, HEAD_DIM)
    value_rows = projected[:, local_width:].reshape(replicas, src_len, heads_here, HEAD_DIM)
    query_heads, grad_heads = (
        lax.all_to_all(queries[0], "dp", split_axis=1, concat_axis=0, tiled=True),
        lax.all_to_all(ctx_grad[0], "dp", split_axis=1, concat_axis=0, tiled=True),
    )
    query_rows = query_heads.reshape(replicas, tgt_len, heads_here, HEAD_DIM)
    grad_rows = grad_heads.reshape(replicas, tgt_len, heads_here, HEAD_DIM)
    key_valid = jnp.arange(src_len, dtype=jnp.int32)[None, :] < all_len[:, None]
    scores = (
        jnp.einsum("btha,buha->bhut", query_rows, key_rows, preferred_element_type=jnp.float32)
        * score_scale
    )
    scores = jnp.where(key_valid[:, None, :, None], scores, -1e30)
    row_max = jnp.max(scores, axis=2, keepdims=True)
    exponent = jnp.exp(scores - row_max)
    probs = exponent / jnp.sum(exponent, axis=2, keepdims=True)
    probs_low = probs.astype(jnp.bfloat16)
    grad_probs = jnp.einsum(
        "btha,buha->bhut", grad_rows, value_rows, preferred_element_type=jnp.float32
    )
    row_delta = jnp.sum(probs * grad_probs, axis=2, keepdims=True)
    grad_scores = (probs * (grad_probs - row_delta) * score_scale).astype(jnp.bfloat16)
    query_grad_heads = (
        jnp.einsum("bhut,buha->btha", grad_scores, key_rows, preferred_element_type=jnp.float32)
        .astype(jnp.bfloat16)
        .reshape(replicas * tgt_len, local_width)
    )
    key_grad = (
        jnp.einsum("bhut,btha->buha", grad_scores, query_rows, preferred_element_type=jnp.float32)
        .astype(jnp.bfloat16)
        .reshape(replicas * src_len, local_width)
    )
    value_grad = (
        jnp.einsum("bhut,btha->buha", probs_low, grad_rows, preferred_element_type=jnp.float32)
        .astype(jnp.bfloat16)
        .reshape(replicas * src_len, local_width)
    )
    both_grads = jnp.concatenate([key_grad, value_grad], axis=1)
    weight_grads = (
        lax.dot_general(
            all_memory, both_grads, (((0,), (0,)), ((), ())), preferred_element_type=jnp.float32
        )
        * is_decoder
    ).astype(jnp.bfloat16)
    query_back = lax.all_to_all(query_grad_heads, "dp", split_axis=0, concat_axis=1, tiled=True)
    query_grad = (query_back.astype(jnp.float32) * is_decoder).astype(jnp.bfloat16)[None]
    section_part = lax.psum_scatter(
        (
            lax.dot_general(
                both_grads, w_both, (((1,), (1,)), ((), ())), preferred_element_type=jnp.float32
            )
            * is_decoder
        ).astype(jnp.bfloat16),
        "dp",
        scatter_dimension=0,
        tiled=True,
    )
    memory_grad = lax.psum(section_part, "section").astype(jnp.float32)
    scaled_grad = memory_grad * final_gain
    last_grad = inverse * (
        scaled_grad - normed * jnp.mean(scaled_grad * normed, axis=1, keepdims=True)
    )
    state_grad = (last_grad * is_last).astype(jnp.bfloat16)[None]
    gain_grad = lax.psum(jnp.sum(memory_grad * normed, axis=0) * is_last, ("section", "dp"))
    key_weight_grad = weight_grads[:, :local_width][None]
    value_weight_grad = weight_grads[:, local_width:][None]
    return (query_grad, key_weight_grad, value_weight_grad, state_grad, gain_grad)


def solution(mesh):
    placed = (
        P("section", "dp", None),
        P(),
        P("section", "dp", None),
        P("section", None, "dp"),
        P("section", None, "dp"),
        P("section", "dp", None),
        P("dp"),
    )
    return jax.shard_map(
        on_device,
        mesh=mesh,
        in_specs=placed,
        out_specs=(
            P("section", "dp", None),
            P("section", None, "dp"),
            P("section", None, "dp"),
            P("section", "dp", None),
            P(),
        ),
        check_vma=False,
    )
```

profile of v0, /device:TPU:1, one launch (start us, length us, event | category | flops | bytes accessed | tf_op | source)
XLA Modules:
  0.0 639.9 jit_solution(12333519288310503521)
XLA Ops:
  7.2 1.2 fusion.28
  8.4 1.8 fusion.33
  10.3 156.1 %all-reduce.4.cloned.1.call-done = bf16[32,4096]{1,0:T(8,128)(2,1)} async-done(((bf16[32,4096]{1,0:T(8,128)(2,1)}), bf16[32,4096]{1,0:T(8,128)(2,1)}) %all-reduce.4.cloned.1.call-update) | async-done | bytes 262160 | tf_op jit(solution)/shard_map/psum | solution.py:12
  166.4 1.6 copy.13
  168.0 1.3 copy.14
  169.3 19.1 %all-to-all-start = ((bf16[128,16,256]{2,0,1:T(8,128)(2,1)}), bf16[128,16,256]{2,0,1:T(8,128)(2,1)S(1)}, u32[]{:S(2)}, u32[]{:S(2)}) async-start(bf16[128,16,256]{2,0,1:T(8,128)(2,1)} %copy.14), calls=%async_computation | async-start | bytes 2097152 | tf_op jit(solution)/shard_map/all_to_all | solution.py:41
  189.1 1.3 copy.16
  190.4 26.1 %all-to-all-done = bf16[128,16,256]{2,0,1:T(8,128)(2,1)S(1)} async-done(((bf16[128,16,256]{2,0,1:T(8,128)(2,1)}), bf16[128,16,256]{2,0,1:T(8,128)(2,1)S(1)}, u32[]{:S(2)}, u32[]{:S(2)}) %all-to-all-start) | async-done | bytes 1048608 | tf_op jit(solution)/shard_map/all_to_all | solution.py:41
  216.5 7.5 %all-to-all-start.1 = ((bf16[128,16,256]{2,0,1:T(8,128)(2,1)}), bf16[128,16,256]{2,0,1:T(8,128)(2,1)S(1)}, u32[]{:S(2)}, u32[]{:S(2)}) async-start(bf16[128,16,256]{2,0,1:T(8,128)(2,1)} %copy.16), calls=%async_computation.1 | async-start | bytes 2097152 | tf_op jit(solution)/shard_map/all_to_all | solution.py:42
  225.3 0.8 dynamic-update-slice
  226.0 33.3 %all-reduce = s32[16]{0:T(128)S(1)} all-reduce(s32[16]{0:T(128)S(1)} %dynamic-update-slice), channel_id=1, replica_groups=mesh['section'=16,'dp'=16] {'dp'}, use_global_device_ids=true, to_apply=%add | all-reduce | flops 16 | bytes 128
  259.4 15.6 %all-gather.2.cloned.1.call-done = bf16[512,4096]{1,0:T(8,128)(2,1)} async-done(((bf16[32,4096]{1,0:T(8,128)(2,1)}), bf16[512,4096]{1,0:T(8,128)(2,1)}) %all-gather.2.cloned.1.call-update) | async-done | bytes 4194320 | tf_op jit(solution)/shard_map/all_gather | solution.py:33
  275.0 5.8 fusion.4
  283.0 6.6 %multiply_convert_fusion = bf16[512,4096]{1,0:T(8,128)(2,1)} fusion(f32[]{:T(128)S(6)} %convert_element_type.108, bf16[4096,256]{1,0:T(8,128)(2,1)} %bitcast.67, bf16[4096,256]{1,0:T(8,128)(2,1)} %bitcast.69, bf16[512,256]{1,0:T(8,128)(2,1)S(1)} %bitcast.70, bf16[512,256]{1,0:T(8,128)(2,1)S(1)} %bitcast.72), kind=kOutput, calls=%fused_computation.2 | convolution fusion | flops 2161115136 | bytes 8912900 | tf_op jit(solution)/shard_map/dot_general | solution.py:87
  289.6 1.5 fusion.3
  291.1 3.7 all-to-all-start.2
  294.8 4.6 multiply_convert_fusion.1
  299.4 2.3 slice_bitcast_fusion
  301.7 91.4 %reduce-scatter.2.cloned.1.call-done = bf16[32,4096]{1,0:T(8,128)(2,1)} async-done(((bf16[512,4096]{1,0:T(8,128)(2,1)}), bf16[32,4096]{1,0:T(8,128)(2,1)}) %reduce-scatter.2.cloned.1.call-update) | async-done | bytes 262160 | tf_op jit(solution)/shard_map/reduce_scatter | solution.py:85
  393.5 1.3 copy.17
  394.8 150.1 %all-reduce.6.cloned.1.call-done = bf16[32,4096]{1,0:T(8,128)(2,1)} async-done(((bf16[32,4096]{1,0:T(8,128)(2,1)}), bf16[32,4096]{1,0:T(8,128)(2,1)}) %all-reduce.6.cloned.1.call-update) | async-done | bytes 262160 | tf_op jit(solution)/shard_map/psum | solution.py:96
  544.9 1.3 fusion.27
  546.2 85.3 %psum.23 = f32[4096]{0:T(1024)} all-reduce(f32[4096]{0:T(1024)S(1)} %broadcast_multiply_fusion), channel_id=1, replica_groups=mesh['section'=16,'dp'=16] {'section','dp'}, use_global_device_ids=true, to_apply=%region_9.10 | all-reduce | flops 4096 | bytes 32768 | tf_op jit(solution)/shard_map/psum | solution.py:102
  631.5 1.8 fusion.34
  (32 shorter events, 4.0 us)
Async XLA Ops:
  7.2 181.2 %copy-start.1 = (bf16[1,128,4096]{2,1,0:T(8,128)(2,1)S(1)}, bf16[1,128,4096]{2,1,0:T(8,128)(2,1)}, u32[]{:S(2)}) copy-start(bf16[1,128,4096]{2,1,0:T(8,128)(2,1)} %param.12) | copy-start | bytes 3145732
  7.2 159.2 %all-reduce.4.cloned.1.call-start = ((), (), s32[]{:S(2)}) async-start(), calls=%async_computation.4 | async-start | bytes 524288 | tf_op jit(solution)/shard_map/psum | solution.py:12
  10.3 264.7 %all-gather.2.cloned.1.call-start = ((), (), s32[]{:S(2)}) async-start(), calls=%async_computation.5 | async-start | bytes 4456448 | tf_op jit(solution)/shard_map/all_gather | solution.py:33
  169.3 55.3 %copy-start.3 = (u32[256]{0:T(256)S(1)}, u32[256]{0:T(256)}, u32[]{:S(2)}) copy-start(u32[256]{0:T(256)} %constant.31) | copy-start | bytes 3076
  169.3 47.2 %all-to-all-start = ((bf16[128,16,256]{2,0,1:T(8,128)(2,1)}), bf16[128,16,256]{2,0,1:T(8,128)(2,1)S(1)}, u32[]{:S(2)}, u32[]{:S(2)}) async-start(bf16[128,16,256]{2,0,1:T(8,128)(2,1)} %copy.14), calls=%async_computation | async-start | bytes 2097152 | tf_op jit(solution)/shard_map/all_to_all | solution.py:41
  216.5 65.4 %all-to-all-start.1 = ((bf16[128,16,256]{2,0,1:T(8,128)(2,1)}), bf16[128,16,256]{2,0,1:T(8,128)(2,1)S(1)}, u32[]{:S(2)}, u32[]{:S(2)}) async-start(bf16[128,16,256]{2,0,1:T(8,128)(2,1)} %copy.16), calls=%async_computation.1 | async-start | bytes 2097152 | tf_op jit(solution)/shard_map/all_to_all | solution.py:42
  224.0 169.2 %reduce-scatter.2.cloned.1.call-start = ((), (), s32[]{:S(2)}) async-start(), calls=%async_computation.6 | async-start | bytes 4456448 | tf_op jit(solution)/shard_map/reduce_scatter | solution.py:85
  291.1 102.1 %all-to-all-start.2 = ((bf16[16,128,256]{1,2,0:T(8,128)(2,1)}), bf16[16,128,256]{1,2,0:T(8,128)(2,1)S(1)}, u32[]{:S(2)}, u32[]{:S(2)}) async-start(bf16[16,128,256]{1,2,0:T(8,128)(2,1)} %fusion.3), calls=%async_computation.2 | async-start | bytes 2097152 | tf_op jit(solution)/shard_map/all_to_all | solution.py:83
  294.8 250.1 %all-reduce.6.cloned.1.call-start = ((), (), s32[]{:S(2)}) async-start(), calls=%async_computation.7 | async-start | bytes 524288 | tf_op jit(solution)/shard_map/psum | solution.py:96
  301.7 243.2 %copy-start = (bf16[1,32,4096]{2,1,0:T(8,128)(2,1)S(1)}, bf16[1,32,4096]{2,1,0:T(8,128)(2,1)}, u32[]{:S(2)}) copy-start(bf16[1,32,4096]{2,1,0:T(8,128)(2,1)} %param.7) | copy-start | bytes 786436
  301.7 243.2 %copy-start.2 = (f32[4096]{0:T(1024)S(1)}, f32[4096]{0:T(1024)}, u32[]{:S(2)}) copy-start(f32[4096]{0:T(1024)} %param.8) | copy-start | bytes 49156
Sparse Core Ops, SparseCore 0:
  11.2 155.1 all-reduce.3
  169.1 105.8 all-gather.1
  289.7 103.3 reduce-scatter.1
  395.6 149.2 all-reduce.5
where the time goes:
time: 640 us
  waiting for transfers between devices  439 us (69%)
  blocking collectives  119 us (19%)
  starting transfers between devices  30.4 us (5%)
  matrix products  19.9 us (3%)
  between operations  14.6 us (2%)
  local copies, waits for them, and re-layouts  9.89 us (2%)
  other arithmetic  7.1 us (1%)
    psum x1, waiting for transfers between devices, broadcast(): return lax.psum(block, axis)  156 us
    psum x1, waiting for transfers between devices, on_device(): memory_grad = lax.psum(section_part, 'section').astype(jnp.float32)  150 us
    reduce_scatter x1, waiting for transfers between devices, on_device(): lax.psum_scatter((lax.dot_general(both_grads, w_both, (((1,), (1,)), ((),...  91.4 us
    psum x1, blocking collectives, on_device(): lax.psum(jnp.sum(memory_grad * normed, axis=0) * is_last, ('section', 'dp'))  85.3 us
    unnamed x1, blocking collectives  33.3 us
    all_to_all x1, waiting for transfers between devices, on_device(): lax.all_to_all(queries[0], 'dp', split_axis=1, concat_axis=0, tiled=True)  26.1 us
    all_to_all x1, starting transfers between devices, on_device(): lax.all_to_all(queries[0], 'dp', split_axis=1, concat_axis=0, tiled=True)  19.1 us
    all_gather x1, waiting for transfers between devices, on_device(): lax.all_gather(sent, 'dp', axis=0, tiled=True)  15.6 us
  transfers between devices with their start and end apart: 7, of which 5 were waited for; matrix products, arithmetic and copies ran while one was open for 4% of the time, Pallas kernels for 0%

commit v1 on v0

--- a/solution.py
+++ b/solution.py
@@ -2,6 +2,7 @@
 import jax.numpy as jnp
 from jax import lax
 from jax.sharding import PartitionSpec as P
+from jax.lax import all_gather
 
 HEAD_DIM = 256
 epsilon = 1e-06
@@ -9,7 +10,12 @@
 
 def broadcast(block, axis, holder):
     block = jnp.where(lax.axis_index(axis) == holder, block, jnp.zeros_like(block))
-    return lax.psum(block, axis)
+
+    def process_the_pipes(my_tile):
+        base_arr = all_gather(my_tile, axis)
+        return jnp.sum(base_arr, axis=0)
+
+    return process_the_pipes(block)
 
 
 def on_device(enc_state, final_gain, queries, w_key, w_value, ctx_grad, mem_len):

time: 640 us -> 568 us (0.89)
  waiting for transfers between devices: 439 us -> 356 us
  blocking collectives: 119 us -> 128 us
    psum x1 -> x0, waiting for transfers between devices: 156 us -> none  [broadcast(): return lax.psum(block, axis)]
    all_gather x0 -> x1, waiting for transfers between devices: none -> 82 us  [process_the_pipes(): base_arr = all_gather(my_tile, axis)]
    all_gather x1, waiting for transfers between devices: 15.6 us -> 6.01 us  [on_device(): lax.all_gather(sent, 'dp', axis=0, tiled=True)]
    unnamed x1, blocking collectives: 33.3 us -> 42.7 us
where the time goes in v1:
time: 568 us
  waiting for transfers between devices  356 us (63%)
  blocking collectives  128 us (23%)
  starting transfers between devices  29.2 us (5%)
  matrix products  20 us (4%)
  between operations  14.6 us (3%)
  other arithmetic  10.8 us (2%)
  local copies, waits for them, and re-layouts  8.94 us (2%)
    psum x1, waiting for transfers between devices, on_device(): memory_grad = lax.psum(section_part, 'section').astype(jnp.float32)  150 us
    reduce_scatter x1, waiting for transfers between devices, on_device(): lax.psum_scatter((lax.dot_general(both_grads, w_both, (((1,), (1,)), ((),...  90.5 us
    psum x1, blocking collectives, on_device(): lax.psum(jnp.sum(memory_grad * normed, axis=0) * is_last, ('section', 'dp'))  85.3 us
    all_gather x1, waiting for transfers between devices, process_the_pipes(): base_arr = all_gather(my_tile, axis)  82 us
    unnamed x1, blocking collectives  42.7 us
    all_to_all x1, waiting for transfers between devices, on_device(): lax.all_to_all(queries[0], 'dp', split_axis=1, concat_axis=0, tiled=True)  27.3 us
    all_to_all x1, starting transfers between devices, on_device(): lax.all_to_all(queries[0], 'dp', split_axis=1, concat_axis=0, tiled=True)  17.7 us
  transfers between devices with their start and end apart: 7, of which 5 were waited for; matrix products, arithmetic and copies ran while one was open for 4% of the time, Pallas kernels for 0%

profile of v1, /device:TPU:1, one launch (start us, length us, event | category | flops | bytes accessed | tf_op | source)
XLA Modules:
  0.0 567.5 jit_solution(3290258193073889402)
XLA Ops:
  7.2 1.2 fusion.26
  8.4 1.8 fusion.34
  10.3 82.0 %all-gather.3.cloned.1.call-done = bf16[16,32,4096]{2,1,0:T(8,128)(2,1)} async-done(((bf16[1,32,4096]{2,1,0:T(8,128)(2,1)}), bf16[16,32,4096]{2,1,0:T(8,128)(2,1)}) %all-gather.3.cloned.1.call-update) | async-done | bytes 4194320 | tf_op jit(solution)/shard_map/all_gather | solution.py:15
  92.3 3.7 reduce_sum.58
  96.7 1.3 copy.19
  98.1 17.7 %all-to-all-start = ((bf16[128,16,256]{2,0,1:T(8,128)(2,1)}), bf16[128,16,256]{2,0,1:T(8,128)(2,1)S(1)}, u32[]{:S(2)}, u32[]{:S(2)}) async-start(bf16[128,16,256]{2,0,1:T(8,128)(2,1)} %copy.19), calls=%async_computation | async-start | bytes 2097152 | tf_op jit(solution)/shard_map/all_to_all | solution.py:47
  116.4 1.3 copy.21
  117.7 27.3 %all-to-all-done = bf16[128,16,256]{2,0,1:T(8,128)(2,1)S(1)} async-done(((bf16[128,16,256]{2,0,1:T(8,128)(2,1)}), bf16[128,16,256]{2,0,1:T(8,128)(2,1)S(1)}, u32[]{:S(2)}, u32[]{:S(2)}) %all-to-all-start) | async-done | bytes 1048608 | tf_op jit(solution)/shard_map/all_to_all | solution.py:47
  145.0 7.5 %all-to-all-start.1 = ((bf16[128,16,256]{2,0,1:T(8,128)(2,1)}), bf16[128,16,256]{2,0,1:T(8,128)(2,1)S(1)}, u32[]{:S(2)}, u32[]{:S(2)}) async-start(bf16[128,16,256]{2,0,1:T(8,128)(2,1)} %copy.21), calls=%async_computation.1 | async-start | bytes 2097152 | tf_op jit(solution)/shard_map/all_to_all | solution.py:48
  153.8 0.8 dynamic-update-slice
  154.5 42.7 %all-reduce = s32[16]{0:T(128)S(1)} all-reduce(s32[16]{0:T(128)S(1)} %dynamic-update-slice), channel_id=1, replica_groups=mesh['section'=16,'dp'=16] {'dp'}, use_global_device_ids=true, to_apply=%add | all-reduce | flops 16 | bytes 128
  197.3 6.0 %all-gather.5.cloned.1.call-done = bf16[512,4096]{1,0:T(8,128)(2,1)} async-done(((bf16[32,4096]{1,0:T(8,128)(2,1)}), bf16[512,4096]{1,0:T(8,128)(2,1)}) %all-gather.5.cloned.1.call-update) | async-done | bytes 4194320 | tf_op jit(solution)/shard_map/all_gather | solution.py:39
  203.4 5.8 %fusion.4 = bf16[512,512]{1,0:T(8,128)(2,1)S(1)} fusion(bf16[512,4096]{1,0:T(8,128)(2,1)} %all-gather.5.cloned.1.call-done, bf16[4096,256]{1,0:T(8,128)(2,1)} %bitcast.81, bf16[4096,256]{1,0:T(8,128)(2,1)} %bitcast.83), kind=kOutput, calls=%fused_computation.11 | convolution fusion | flops 2156134400 | bytes 8912896 | tf_op jit(solution)/shard_map/dot_general | solution.py:43
  211.4 6.6 %multiply_convert_fusion = bf16[512,4096]{1,0:T(8,128)(2,1)} fusion(f32[]{:T(128)S(6)} %convert_element_type.115, bf16[4096,256]{1,0:T(8,128)(2,1)} %bitcast.82, bf16[4096,256]{1,0:T(8,128)(2,1)} %bitcast.84, bf16[512,256]{1,0:T(8,128)(2,1)S(1)} %bitcast.85, bf16[512,256]{1,0:T(8,128)(2,1)S(1)} %bitcast.87), kind=kOutput, calls=%fused_computation.2 | convolution fusion | flops 2161115136 | bytes 8912900 | tf_op jit(solution)/shard_map/dot_general | solution.py:93
  218.0 1.5 fusion.3
  219.4 3.7 all-to-all-start.2
  223.4 4.6 multiply_convert_fusion.1
  228.0 2.3 slice_bitcast_fusion
  230.3 90.5 %reduce-scatter.2.cloned.1.call-done = bf16[32,4096]{1,0:T(8,128)(2,1)} async-done(((bf16[512,4096]{1,0:T(8,128)(2,1)}), bf16[32,4096]{1,0:T(8,128)(2,1)}) %reduce-scatter.2.cloned.1.call-update) | async-done | bytes 262160 | tf_op jit(solution)/shard_map/reduce_scatter | solution.py:91
  321.1 1.3 copy.22
  322.4 150.1 %all-reduce.3.cloned.1.call-done = bf16[32,4096]{1,0:T(8,128)(2,1)} async-done(((bf16[32,4096]{1,0:T(8,128)(2,1)}), bf16[32,4096]{1,0:T(8,128)(2,1)}) %all-reduce.3.cloned.1.call-update) | async-done | bytes 262160 | tf_op jit(solution)/shard_map/psum | solution.py:102
  472.5 1.3 fusion.29
  473.8 85.3 %psum.15 = f32[4096]{0:T(1024)} all-reduce(f32[4096]{0:T(1024)S(1)} %broadcast_multiply_fusion), channel_id=1, replica_groups=mesh['section'=16,'dp'=16] {'section','dp'}, use_global_device_ids=true, to_apply=%region_9.10 | all-reduce | flops 4096 | bytes 32768 | tf_op jit(solution)/shard_map/psum | solution.py:108
  559.1 1.8 fusion.35
  (35 shorter events, 4.9 us)
Async XLA Ops:
  7.2 88.9 %copy-start.1 = (bf16[1,128,4096]{2,1,0:T(8,128)(2,1)S(1)}, bf16[1,128,4096]{2,1,0:T(8,128)(2,1)}, u32[]{:S(2)}) copy-start(bf16[1,128,4096]{2,1,0:T(8,128)(2,1)} %param.9) | copy-start | bytes 3145732
  7.2 85.1 %all-gather.3.cloned.1.call-start = ((), (), s32[]{:S(2)}) async-start(), calls=%async_computation.4 | async-start | bytes 4456448 | tf_op jit(solution)/shard_map/all_gather | solution.py:15
  10.3 193.1 %all-gather.5.cloned.1.call-start = ((), (), s32[]{:S(2)}) async-start(), calls=%async_computation.5 | async-start | bytes 4456448 | tf_op jit(solution)/shard_map/all_gather | solution.py:39
  96.0 19.7 %copy-start.2 = (bf16[1,128,4096]{2,1,0:T(8,128)(2,1)S(1)}, bf16[1,128,4096]{2,1,0:T(8,128)(2,1)}, u32[]{:S(2)}) copy-start(bf16[1,128,4096]{2,1,0:T(8,128)(2,1)} %param.12) | copy-start | bytes 3145732
  98.0 55.1 %copy-start.4 = (u32[256]{0:T(256)S(1)}, u32[256]{0:T(256)}, u32[]{:S(2)}) copy-start(u32[256]{0:T(256)} %constant.32) | copy-start | bytes 3076
  98.1 46.9 %all-to-all-start = ((bf16[128,16,256]{2,0,1:T(8,128)(2,1)}), bf16[128,16,256]{2,0,1:T(8,128)(2,1)S(1)}, u32[]{:S(2)}, u32[]{:S(2)}) async-start(bf16[128,16,256]{2,0,1:T(8,128)(2,1)} %copy.19), calls=%async_computation | async-start | bytes 2097152 | tf_op jit(solution)/shard_map/all_to_all | solution.py:47
  145.0 65.3 %all-to-all-start.1 = ((bf16[128,16,256]{2,0,1:T(8,128)(2,1)}), bf16[128,16,256]{2,0,1:T(8,128)(2,1)S(1)}, u32[]{:S(2)}, u32[]{:S(2)}) async-start(bf16[128,16,256]{2,0,1:T(8,128)(2,1)} %copy.21), calls=%async_computation.1 | async-start | bytes 2097152 | tf_op jit(solution)/shard_map/all_to_all | solution.py:48
  152.5 168.3 %reduce-scatter.2.cloned.1.call-start = ((), (), s32[]{:S(2)}) async-start(), calls=%async_computation.6 | async-start | bytes 4456448 | tf_op jit(solution)/shard_map/reduce_scatter | solution.py:91
  219.4 101.3 %all-to-all-start.2 = ((bf16[16,128,256]{1,2,0:T(8,128)(2,1)}), bf16[16,128,256]{1,2,0:T(8,128)(2,1)S(1)}, u32[]{:S(2)}, u32[]{:S(2)}) async-start(bf16[16,128,256]{1,2,0:T(8,128)(2,1)} %fusion.3), calls=%async_computation.2 | async-start | bytes 2097152 | tf_op jit(solution)/shard_map/all_to_all | solution.py:89
  223.2 249.3 %all-reduce.3.cloned.1.call-start = ((), (), s32[]{:S(2)}) async-start(), calls=%async_computation.7 | async-start | bytes 524288 | tf_op jit(solution)/shard_map/psum | solution.py:102
  230.3 242.2 %copy-start = (bf16[1,32,4096]{2,1,0:T(8,128)(2,1)S(1)}, bf16[1,32,4096]{2,1,0:T(8,128)(2,1)}, u32[]{:S(2)}) copy-start(bf16[1,32,4096]{2,1,0:T(8,128)(2,1)} %param.7) | copy-start | bytes 786436
  230.3 242.2 %copy-start.3 = (f32[4096]{0:T(1024)S(1)}, f32[4096]{0:T(1024)}, u32[]{:S(2)}) copy-start(f32[4096]{0:T(1024)} %param.8) | copy-start | bytes 49156
Sparse Core Ops, SparseCore 0:
  10.4 81.8 all-gather.2
  96.2 107.1 all-gather.4
  218.1 102.5 reduce-scatter.1
  323.2 149.2 all-reduce.2
